TPU v7x, 128 devices: a whole 4x4x4 slice. The times are simulated.
128 devices in a mesh: tm: 32 (over y_lo, z, x), row: 4 (over y_hi, core).
Axes of the slice: x: 4, y: 4 (y_hi: 2, y_lo: 2; y = y_hi * 2 + y_lo), z: 4, core: 2. Of those that a mesh axis runs over, the one named last changes fastest.
Arguments:
- inputs: bfloat16 [1, 2048, 16, 16, 256], P(None, 'tm', 'row'), may hold values from -6 to 6
- decays: float32 [2048, 256], P('tm'), may hold values from 0.4 to 0.999999, as said below
- in_kernel: bfloat16 [3, 3, 256, 256], replicated, may hold values from -0.125 to 0.125
- out_kernel: bfloat16 [3, 3, 256, 256], replicated, may hold values from -0.125 to 0.125
- skip: float32 [256], replicated, may hold values from -1 to 1
- cotangent: bfloat16 [1, 2048, 16, 16, 256], P(None, 'tm', 'row'), may hold values from -6 to 6
Outputs:
- outputs: bfloat16 [1, 2048, 16, 16, 256], P(None, 'tm', 'row')
- in_kernel_grad: float32 [3, 3, 256, 256], replicated
- out_kernel_grad: float32 [3, 3, 256, 256], replicated
Inputs may be any that keep to these rules, and one draw needn't show every extreme that they name: `decays`: strictly below one.
All inputs are finite; a program needn't handle non-finite values.
Results may differ from a plain program's by a relative error of at most 0.0043.
Values may be sent and summed in bfloat16 or wider, within the bound.
A program may use at most 128 MiB of HBM per device.

v0:
```python
import math

import jax
import jax.numpy as jnp
from jax import lax
from jax.sharding import PartitionSpec as P


def padded_2(cells, sides, width):
    for axis, dim in sides:
        count = lax.axis_size(axis)
        ends = count - 1
        head = lax.slice_in_dim(cells, 0, width, axis=dim)
        tail = lax.slice_in_dim(cells, cells.shape[dim] - width, cells.shape[dim], axis=dim)
        cells = jnp.concatenate(
            [
                lax.ppermute(tail, axis, [(i, (i + 1) % count) for i in range(ends)]),
                cells,
                lax.ppermute(head, axis, [((i + 1) % count, i) for i in range(ends)]),
            ],
            axis=dim,
        )
    return cells


def passed_along(shard, axis, by):
    count = lax.axis_size(axis)
    pairs = [(i, i + by) for i in range(count) if 0 <= i + by < count]
    return lax.ppermute(shard, axis, pairs)


def conv_rows(padded, kernel):
    return lax.conv_general_dilated(
        padded,
        kernel,
        (1, 1),
        ((0, 0), (1, 1)),
        dimension_numbers=("NHWC", "HWIO", "NHWC"),
        preferred_element_type=jnp.float32,
    )


def linear_combine(earlier, following):
    return (earlier[0] * following[0], following[0] * earlier[1] + following[1])


def expand(per_frame):
    return per_frame[None, :, None, None, :]


def local_recurrence(factors, terms):
    return lax.associative_scan(
        linear_combine, (jnp.broadcast_to(factors, terms.shape), terms), axis=1
    )[1]


def tap_grads(padded, cotan_flat):
    lines_per_shard = cotan_flat.shape[1]
    width_dev = cotan_flat.shape[2]
    collected = []
    for tap_row in range(3):
        for tap_col in range(3):
            window = padded[
                :, tap_row : tap_row + lines_per_shard, tap_col : tap_col + width_dev, :
            ]
            collected.append(
                lax.dot_general(
                    window,
                    cotan_flat,
                    (((0, 1, 2), (0, 1, 2)), ((), ())),
                    preferred_element_type=jnp.float32,
                )
            )
    return jnp.stack(collected).reshape(3, 3, padded.shape[3], cotan_flat.shape[3])


def per_device(inputs, decays, in_kernel, out_kernel, skip, cotangent):
    clips_dev, frames_dev, lines_per_shard, width_dev, channels = inputs.shape
    hidden_state_width = in_kernel.shape[3]
    batch_rows = clips_dev * frames_dev
    frames_all = frames_dev * lax.axis_size("tm")
    height = lines_per_shard * lax.axis_size("row")
    grad_scale = 1.0 / math.sqrt(clips_dev * frames_all * height * width_dev)
    latent_memory_dims = (clips_dev, frames_dev, lines_per_shard, width_dev, hidden_state_width)
    column_pad = ((0, 0), (0, 0), (1, 1), (0, 0))
    flat_in = inputs.reshape(batch_rows, lines_per_shard, width_dev, channels)
    in_rim = padded_2(flat_in, (("row", 1),), 1)
    scale_in = jnp.sqrt((1.0 - decays) * (1.0 + decays))
    drive = conv_rows(in_rim, in_kernel).reshape(latent_memory_dims)
    local_states = local_recurrence(expand(decays), expand(scale_in) * drive)
    running = jnp.cumprod(decays, axis=0)
    block_decay = running[-1]
    block_end = local_states[:, -1]

    def forward_pass(position, incoming):
        return passed_along(block_decay * incoming + block_end, "tm", 1)

    incoming = lax.fori_loop(0, lax.axis_size("tm") - 1, forward_pass, jnp.zeros_like(block_end))
    states = local_states + expand(running) * incoming[:, None]
    flat_state = states.astype(jnp.bfloat16).reshape(
        batch_rows, lines_per_shard, width_dev, hidden_state_width
    )
    state_rim = padded_2(flat_state, (("row", 1),), 1)
    mixed_out = conv_rows(state_rim, out_kernel).reshape(inputs.shape)
    outputs = (mixed_out + skip * inputs.astype(jnp.float32)).astype(jnp.bfloat16)
    flat_cot = cotangent.reshape(batch_rows, lines_per_shard, width_dev, channels)
    cot_rim = padded_2(flat_cot, (("row", 1),), 1)
    out_grad = tap_grads(jnp.pad(state_rim, column_pad), flat_cot) * grad_scale
    flipped = jnp.transpose(jnp.flip(out_kernel, (0, 1)), (0, 1, 3, 2))
    state_cot = conv_rows(cot_rim, flipped).reshape(latent_memory_dims)
    next_decay = jnp.concatenate([decays[1:], jnp.ones_like(decays[:1])], axis=0)
    reversed_decay = jnp.flip(next_decay, 0)
    reverse_local = jnp.flip(local_recurrence(expand(reversed_decay), jnp.flip(state_cot, 1)), 1)
    trailing = jnp.flip(jnp.cumprod(reversed_decay, axis=0), 0)
    leading = decays[0] * reverse_local[:, 0]

    def backward_pass(position, arriving):
        return passed_along(block_decay * arriving + leading, "tm", -1)

    arriving = lax.fori_loop(0, lax.axis_size("tm") - 1, backward_pass, jnp.zeros_like(leading))
    adjoint = reverse_local + expand(trailing) * arriving[:, None]
    drive_cot = (
        (expand(scale_in) * adjoint)
        .astype(jnp.bfloat16)
        .reshape(batch_rows, lines_per_shard, width_dev, hidden_state_width)
    )
    in_grad = tap_grads(jnp.pad(in_rim, column_pad), drive_cot) * grad_scale
    in_grad, out_grad = lax.psum((in_grad, out_grad), ("tm", "row"))
    return (outputs, in_grad, out_grad)


def solution(mesh):
    return jax.shard_map(
        per_device,
        mesh=mesh,
        in_specs=(
            P(None, "tm", "row", None, None),
            P("tm", None),
            P(),
            P(),
            P(),
            P(None, "tm", "row", None, None),
        ),
        out_specs=(P(None, "tm", "row", None, None), P(), P()),
        check_vma=False,
    )
```

profile of v0, /device:TPU:1, one launch (start us, length us, event | category | flops | bytes accessed | tf_op | source)
XLA Modules:
  0.0 1406.5 jit_solution(10657063552636818331)
XLA Ops:
  48.3 7.8 fusion.1
  62.8 9.8 slice.474
  72.6 9.8 slice.473
  97.9 9.9 slice.515
  149.8 7.5 multiply_bitcast_fusion
  159.9 9.9 slice.459
  169.8 9.8 slice.419
  179.6 9.8 slice.418
  225.5 22.4 %pad.102 = f32[1,16,4,16,256]{4,1,3,2,0:T(8,128)S(1)} pad(f32[1,8,4,16,256]{4,1,3,2,0:T(8,128)} %add.214, f32[]{:T(128)} %constant.14.clone.1), padding=0_0_0x1_0_1x0_0_0x0_0_0x0_0_0 | pad | bytes 1572868 | tf_op jit(solution)/shard_map/pad | solution.py:52
  251.4 23.2 %pad.103 = f32[1,32,4,16,256]{4,1,3,2,0:T(8,128)S(1)} pad(f32[1,16,4,16,256]{4,1,3,2,0:T(8,128)} %pad_maximum_fusion.5, f32[]{:T(128)} %constant.14.clone.1), padding=0_0_0x0_1_1x0_0_0x0_0_0x0_0_0 | pad | bytes 3145732 | tf_op jit(solution)/shard_map/pad | solution.py:52
  274.6 30.7 %pad.104 = f32[1,32,4,16,256]{4,1,3,2,0:T(8,128)} pad(f32[1,16,4,16,256]{4,1,3,2,0:T(8,128)} %add.216, f32[]{:T(128)} %constant.14.clone.1), padding=0_0_0x1_0_1x0_0_0x0_0_0x0_0_0 | pad | bytes 3145732 | tf_op jit(solution)/shard_map/pad | solution.py:52
  311.4 32.6 %pad.105 = f32[1,64,4,16,256]{4,1,3,2,0:T(8,128)} pad(f32[1,32,4,16,256]{4,1,3,2,0:T(8,128)} %pad_maximum_fusion.3, f32[]{:T(128)} %constant.14.clone.1), padding=0_0_0x0_1_1x0_0_0x0_0_0x0_0_0 | pad | bytes 6291460 | tf_op jit(solution)/shard_map/pad | solution.py:52
  344.1 22.2 %pad.106 = f32[1,64,4,16,256]{4,1,3,2,0:T(8,128)} pad(f32[1,32,4,16,256]{4,1,3,2,0:T(8,128)S(1)} %copy-done.4, f32[]{:T(128)} %constant.14.clone.1), padding=0_0_0x1_0_1x0_0_0x0_0_0x0_0_0 | pad | bytes 6291460 | tf_op jit(solution)/shard_map/pad | solution.py:52
  381.0 222.9 %while.21 = (s32[]{:T(128)}, f32[1,4,16,256]{3,2,1,0:T(8,128)S(1)}, f32[1,256]{1,0:T(1,128)S(1)}, f32[1,4,16,256]{3,2,1,0:T(8,128)S(1)}, s32[]{:T(128)}) while((s32[]{:T(128)}, f32[1,4,16,256]{3,2,1,0:T(8,128)S(1)}, f32[1,256]{1,0:T(1,128)S(1)}, f32[1,4,16,256]{3,2,1,0:T(8,128)S(1)}, s32[]{:T(128)}) %tuple.55), condition=%wide.region_5.6_spmd, body=%wide.region_4.5_spmd.sunk | while | flops 32770 | bytes 459877 | solution.py:120
  577.7 7.7 collective-permute-done.1
  586.8 7.5 collective-permute-done.1
  595.5 8.4 collective-permute-done.1
  625.8 22.4 %pad.89 = f32[1,16,4,16,256]{4,1,3,2,0:T(8,128)S(1)} pad(f32[1,8,4,16,256]{4,1,3,2,0:T(8,128)} %add.195, f32[]{:T(128)} %constant.14.clone.1), padding=0_0_0x1_0_1x0_0_0x0_0_0x0_0_0 | pad | bytes 1572868 | tf_op jit(solution)/shard_map/pad | solution.py:52
  651.6 23.2 %pad.90 = f32[1,32,4,16,256]{4,1,3,2,0:T(8,128)S(1)} pad(f32[1,16,4,16,256]{4,1,3,2,0:T(8,128)} %pad_maximum_fusion.4, f32[]{:T(128)} %constant.14.clone.1), padding=0_0_0x0_1_1x0_0_0x0_0_0x0_0_0 | pad | bytes 3145732 | tf_op jit(solution)/shard_map/pad | solution.py:52
  674.8 30.5 %pad.91 = f32[1,32,4,16,256]{4,1,3,2,0:T(8,128)} pad(f32[1,16,4,16,256]{4,1,3,2,0:T(8,128)} %add.197, f32[]{:T(128)} %constant.14.clone.1), padding=0_0_0x1_0_1x0_0_0x0_0_0x0_0_0 | pad | bytes 3145732 | tf_op jit(solution)/shard_map/pad | solution.py:52
  711.4 32.6 %pad.92 = f32[1,64,4,16,256]{4,1,3,2,0:T(8,128)} pad(f32[1,32,4,16,256]{4,1,3,2,0:T(8,128)} %pad_maximum_fusion.2, f32[]{:T(128)} %constant.14.clone.1), padding=0_0_0x0_1_1x0_0_0x0_0_0x0_0_0 | pad | bytes 6291460 | tf_op jit(solution)/shard_map/pad | solution.py:52
  744.0 22.1 %pad.93 = f32[1,64,4,16,256]{4,1,3,2,0:T(8,128)} pad(f32[1,32,4,16,256]{4,1,3,2,0:T(8,128)S(1)} %copy-done.5, f32[]{:T(128)} %constant.14.clone.1), padding=0_0_0x1_0_1x0_0_0x0_0_0x0_0_0 | pad | bytes 6291460 | tf_op jit(solution)/shard_map/pad | solution.py:52
  767.5 275.1 %while.20 = (s32[]{:T(128)}, f32[1,4,16,256]{3,2,1,0:T(8,128)S(1)}, f32[1,256]{1,0:T(1,128)S(1)}, f32[1,4,16,256]{3,2,1,0:T(8,128)S(1)}, s32[]{:T(128)}) while((s32[]{:T(128)}, f32[1,4,16,256]{3,2,1,0:T(8,128)S(1)}, f32[1,256]{1,0:T(1,128)S(1)}, f32[1,4,16,256]{3,2,1,0:T(8,128)S(1)}, s32[]{:T(128)}) %tuple.56), condition=%wide.region_2.3_spmd, body=%wide.region_1.2_spmd.sunk | while | flops 32770 | bytes 459877 | solution.py:98
  784.0 8.1 collective-permute-start
  801.7 7.7 collective-permute-start
  819.1 7.6 collective-permute-start
  828.0 7.6 collective-permute-start
  836.9 7.6 collective-permute-start
  845.9 7.6 collective-permute-start
  854.8 7.9 collective-permute-start
  864.6 7.9 collective-permute-start
  873.8 7.7 collective-permute-start
  882.8 7.6 collective-permute-start
  921.8 7.9 collective-permute-start
  931.1 8.6 collective-permute-start
  949.7 8.2 collective-permute-start
  959.2 8.0 collective-permute-start
  968.5 7.4 collective-permute-start
  977.3 8.4 collective-permute-start
  987.1 7.9 collective-permute-start
  996.3 8.1 collective-permute-start
  1005.7 7.7 collective-permute-start
  1014.8 8.0 collective-permute-start
  1024.1 8.0 collective-permute-start
  1033.4 7.9 collective-permute-start
  1047.4 70.6 %collective-permute-start.4 = (bf16[64,1,16,256]{3,0,2,1:T(8,128)(2,1)S(1)}, bf16[64,1,16,256]{3,0,2,1:T(8,128)(2,1)S(1)}, u32[]{:S(2)}, u32[]{:S(2)}) collective-permute-start(bf16[64,1,16,256]{3,0,2,1:T(8,128)(2,1)S(1)} %get-tuple-element.80), channel_id=1, source_target_pairs={{0,1},{1,2},{2,3},{4,5},{5,6},{6,7},{8,9},{9,10},{10,11},{12,13},{... | collective-permute-start | bytes 1572872 | tf_op jit(solution)/shard_map/ppermute | solution.py:17
  1159.6 7.5 fusion
  1169.6 225.0 %all-reduce.30.cloned.1.call-done = (f32[3,3,256,256]{3,2,1,0:T(8,128)}, f32[3,3,256,256]{3,2,1,0:T(8,128)}) async-done(((f32[3,3,256,256]{3,2,1,0:T(8,128)}, f32[3,3,256,256]{3,2,1,0:T(8,128)}), (f32[3,3,256,256]{3,2,1,0:T(8,128)}, f32[3,3,256,256]{3,2,1,0:T(8,128)})) %all-reduce.30.cloned.1.call-update) | async-done | bytes 4718608 | tf_op jit(solution)/shard_map/psum | solution.py:128
  (502 shorter events, 553.8 us)
Async XLA Ops:
  7.2 1387.4 %all-reduce.30.cloned.1.call-start = ((), (), s32[]{:S(2)}) async-start(), calls=%async_computation | async-start | bytes 9437184 | tf_op jit(solution)/shard_map/psum | solution.py:128
  11.3 138.4 %collective-permute-start.2 = (bf16[64,1,16,256]{3,0,2,1:T(8,128)(2,1)}, bf16[64,1,16,256]{3,0,2,1:T(8,128)(2,1)}, u32[]{:S(2)}, u32[]{:S(2)}) collective-permute-start(bf16[64,1,16,256]{3,0,2,1:T(8,128)(2,1)} %get-tuple-element.82), channel_id=1, source_target_pairs={{0,1},{1,2},{2,3},{4,5},{5,6},{6,7},{8,9},{9,10},{10,11},{12,13},{... | collective-permute-start | bytes 1572872 | tf_op jit(solution)/shard_map/ppermute | solution.py:17
  17.5 132.2 %collective-permute-start.3 = (bf16[64,1,16,256]{3,0,2,1:T(8,128)(2,1)}, bf16[64,1,16,256]{3,0,2,1:T(8,128)(2,1)}, u32[]{:S(2)}, u32[]{:S(2)}) collective-permute-start(bf16[64,1,16,256]{3,0,2,1:T(8,128)(2,1)} %get-tuple-element.83), channel_id=1, source_target_pairs={{1,0},{2,1},{3,2},{5,4},{6,5},{7,6},{9,8},{10,9},{11,10},{13,12},{... | collective-permute-start | bytes 1572872 | tf_op jit(solution)/shard_map/ppermute | solution.py:19
  21.8 26.5 %collective-permute-start.6 = (bf16[64,1,16,256]{3,0,2,1:T(8,128)(2,1)}, bf16[64,1,16,256]{3,0,2,1:T(8,128)(2,1)}, u32[]{:S(2)}, u32[]{:S(2)}) collective-permute-start(bf16[64,1,16,256]{3,0,2,1:T(8,128)(2,1)} %get-tuple-element.78), channel_id=1, source_target_pairs={{0,1},{1,2},{2,3},{4,5},{5,6},{6,7},{8,9},{9,10},{10,11},{12,13},{... | collective-permute-start | bytes 1572872 | tf_op jit(solution)/shard_map/ppermute | solution.py:17
  27.0 21.3 %collective-permute-start.7 = (bf16[64,1,16,256]{3,0,2,1:T(8,128)(2,1)}, bf16[64,1,16,256]{3,0,2,1:T(8,128)(2,1)}, u32[]{:S(2)}, u32[]{:S(2)}) collective-permute-start(bf16[64,1,16,256]{3,0,2,1:T(8,128)(2,1)} %get-tuple-element.79), channel_id=1, source_target_pairs={{1,0},{2,1},{3,2},{5,4},{6,5},{7,6},{9,8},{10,9},{11,10},{13,12},{... | collective-permute-start | bytes 1572872 | tf_op jit(solution)/shard_map/ppermute | solution.py:19
  403.1 7.6 collective-permute-start.1
  445.8 8.1 collective-permute-start.1
  460.8 7.2 collective-permute-start.1
  496.1 7.6 collective-permute-start.1
  503.7 8.0 collective-permute-start.1
  553.7 7.9 collective-permute-start.1
  561.6 7.4 collective-permute-start.1
  569.0 7.3 collective-permute-start.1
  576.4 9.0 collective-permute-start.1
  585.5 8.8 collective-permute-start.1
  594.2 9.7 collective-permute-start.1
  767.5 8.4 collective-permute-start
  775.9 8.1 collective-permute-start
  784.0 9.4 collective-permute-start
  793.4 8.3 collective-permute-start
  801.7 9.0 collective-permute-start
  810.8 8.4 collective-permute-start
  819.1 8.9 collective-permute-start
  828.0 8.9 collective-permute-start
  836.9 8.9 collective-permute-start
  845.9 9.0 collective-permute-start
  854.8 9.7 collective-permute-start
  864.6 9.2 collective-permute-start
  873.8 9.0 collective-permute-start
  882.8 9.0 collective-permute-start
  891.8 8.4 collective-permute-start
  900.2 7.1 collective-permute-start
  907.4 7.4 collective-permute-start
  921.8 9.2 collective-permute-start
  931.1 9.9 collective-permute-start
  941.0 8.7 collective-permute-start
  949.7 9.5 collective-permute-start
  959.2 9.3 collective-permute-start
  968.5 8.8 collective-permute-start
  977.3 9.8 collective-permute-start
  987.1 9.2 collective-permute-start
  996.3 9.4 collective-permute-start
  1005.7 9.0 collective-permute-start
  1014.8 9.3 collective-permute-start
  1024.1 9.3 collective-permute-start
  1033.4 9.2 collective-permute-start
  1047.4 85.1 %collective-permute-start.4 = (bf16[64,1,16,256]{3,0,2,1:T(8,128)(2,1)S(1)}, bf16[64,1,16,256]{3,0,2,1:T(8,128)(2,1)S(1)}, u32[]{:S(2)}, u32[]{:S(2)}) collective-permute-start(bf16[64,1,16,256]{3,0,2,1:T(8,128)(2,1)S(1)} %get-tuple-element.80), channel_id=1, source_target_pairs={{0,1},{1,2},{2,3},{4,5},{5,6},{6,7},{8,9},{9,10},{10,11},{12,13},{... | collective-permute-start | bytes 1572872 | tf_op jit(solution)/shard_map/ppermute | solution.py:17
  1118.0 14.5 %collective-permute-start.5 = (bf16[64,1,16,256]{3,0,2,1:T(8,128)(2,1)S(1)}, bf16[64,1,16,256]{3,0,2,1:T(8,128)(2,1)S(1)}, u32[]{:S(2)}, u32[]{:S(2)}) collective-permute-start(bf16[64,1,16,256]{3,0,2,1:T(8,128)(2,1)S(1)} %get-tuple-element.81), channel_id=1, source_target_pairs={{1,0},{2,1},{3,2},{5,4},{6,5},{7,6},{9,8},{10,9},{11,10},{13,12},{... | collective-permute-start | bytes 1572872 | tf_op jit(solution)/shard_map/ppermute | solution.py:19
  (98 other events, 1623.2 us)
Sparse Core Ops, SparseCore 0:
  1159.1 235.4 all-reduce.29
where the time goes:
time: 1430 us; the launch traced here: 1410 us
  local copies, waits for them, and re-layouts  449 us (31%)
  waiting for transfers between devices  448 us (31%)
  starting transfers between devices  361 us (25%)
  matrix products  69.3 us (5%)
  other arithmetic  62.2 us (4%)
  between operations  15.5 us (1%)
    ppermute x62, starting transfers between devices, passed_along(): return lax.ppermute(shard, axis, pairs)  273 us
    pad x20, local copies, waits for them, and re-layouts, local_recurrence(): lax.associative_scan(linear_combine, (jnp.broadcast_to(factors, terms.sha...  269 us
    psum x1, waiting for transfers between devices, per_device(): in_grad, out_grad = lax.psum((in_grad, out_grad), ('tm', 'row'))  225 us
    ppermute x62, waiting for transfers between devices, passed_along(): return lax.ppermute(shard, axis, pairs)  223 us
    slice x71, local copies, waits for them, and re-layouts, local_recurrence(): lax.associative_scan(linear_combine, (jnp.broadcast_to(factors, terms.sha...  144 us
    ppermute x3, starting transfers between devices, padded_2(): lax.ppermute(tail, axis, [(i, (i + 1) % count) for i in range(ends)])  81.9 us
    dot_general x18, matrix products, tap_grads(): lax.dot_general(window, cotan_flat, (((0, 1, 2), (0, 1, 2)), ((), ())), p...  46.6 us
  transfers between devices with their start and end apart: 69, of which 63 were waited for; matrix products, arithmetic and copies ran while one was open for 10% of the time, Pallas kernels for 0%

commit v1 on v0

v1 whole, which is shorter than its diff:
```python
import functools
import math

import jax
import jax.numpy as jnp
from jax import lax
from jax.experimental import pallas as pl
from jax.experimental.pallas import tpu as pltpu
from jax.sharding import PartitionSpec as P

MESH = pl.DeviceIdType.MESH
F32 = jnp.float32
BF16 = jnp.bfloat16

T = 64
R = 4
W = 16
CH = 256
FB = 16
NB = T // FB
M = FB * W
CELLS = R * W
MSG = CELLS + 8
HALF = 9 * 128
ORDERS = (("x", "z", "y"), ("z", "y", "x"), ("y", "x", "z"))


def column(rows):
    return lax.broadcasted_iota(jnp.int32, (rows, CH), 0) & (W - 1)


def from_left(v):
    return jnp.where(column(v.shape[0]) == 0, 0.0, pltpu.roll(v, 1, 0))


def from_right(v):
    return jnp.where(column(v.shape[0]) == W - 1, 0.0, pltpu.roll(v, v.shape[0] - 1, 0))


def kernel(
    grad_scale,
    x_hbm, dec, kin_hbm, kout_hbm, skip, cot_hbm,
    out_hbm, gin_hbm, gout_hbm,
    xi, ci, kin, kout, ft, drv, adj, sb, dcb, ob, sc,
    rx, rz, ry, incoming,
    acc, gbuf, psend, precv, hbuf, s1, r1, c1, r2, c2, r3, agb, pgb, fb,
    lsem, wsem, osem, gsem,
    hsend, hrecv, xsend, xrecv, zsend, zrecv, ysend, yrecv,
    psem, prem, s1s, s1r, s2s, s2r, s3s, s3r, a2s, a2r, a1s, a1r, pgs, pgr,
):
    tm = lax.axis_index("tm")
    row = lax.axis_index("row")
    core = lax.rem(row, 2)
    y_lo = tm // 16
    pos = {"x": lax.rem(tm, 4), "z": lax.rem(tm // 4, 4), "y": (row // 2) * 2 + y_lo}

    def mate(axis, k):
        if axis == "x":
            return ((tm // 4) * 4 + k, row)
        if axis == "z":
            return (y_lo * 16 + k * 4 + lax.rem(tm, 4), row)
        return (lax.rem(k, 2) * 16 + lax.rem(tm, 16), (k // 2) * 2 + core)

    def step(axis, d):
        return lax.rem(pos[axis] + d, 4)

    pair = (tm, row + 1 - 2 * core)
    up = (tm, row - 1)
    down = (tm, row + 1)

    def remote(src, dst, ssem, rsem, device):
        return pltpu.make_async_remote_copy(
            src_ref=src, dst_ref=dst, send_sem=ssem, recv_sem=rsem,
            device_id=device, device_id_type=MESH,
        )

    mid = pl.ds(CH, CH)
    loads = []
    for r in range(R):
        for n, (hbm, buf) in enumerate(((x_hbm, xi), (cot_hbm, ci))):
            loads.append(pltpu.make_async_copy(hbm.at[:, r], buf.at[r + 1, :, :, mid], lsem.at[n, r]))
    load_kin = pltpu.make_async_copy(kin_hbm, kin, wsem.at[0])
    load_kout = pltpu.make_async_copy(kout_hbm, kout, wsem.at[1])
    load_kout.start()
    for load in loads:
        load.start()
    load_kin.start()

    barrier = pltpu.get_barrier_semaphore()
    for axis in ("x", "z", "y"):
        for d in (1, 2, 3):
            pl.semaphore_signal(barrier, inc=1, device_id=mate(axis, step(axis, d)), device_id_type=MESH)
    pl.semaphore_signal(barrier, inc=1, device_id=pair, device_id_type=MESH)

    @pl.when(row == 1)
    def _():
        pl.semaphore_signal(barrier, inc=1, device_id=down, device_id_type=MESH)
        pl.semaphore_wait(barrier, 11)

    @pl.when(row == 2)
    def _():
        pl.semaphore_signal(barrier, inc=1, device_id=up, device_id_type=MESH)
        pl.semaphore_wait(barrier, 11)

    @pl.when((row == 0) | (row == 3))
    def _():
        pl.semaphore_wait(barrier, 10)

    def halo(n, way):
        if n == 2:
            src = sb.at[1] if way == 0 else sb.at[R]
            dst = sb.at[R + 1] if way == 0 else sb.at[0]
        else:
            hbm, buf = ((x_hbm, xi), (cot_hbm, ci))[n]
            src = hbm.at[:, 0] if way == 0 else hbm.at[:, R - 1]
            dst = buf.at[R + 1, :, :, mid] if way == 0 else buf.at[0, :, :, mid]
        return remote(src, dst, hsend.at[n, way], hrecv.at[n, way], up if way == 0 else down)

    def halo_start(n):
        @pl.when(row > 0)
        def _():
            halo(n, 0).start()

        @pl.when(row < 3)
        def _():
            halo(n, 1).start()

    def halo_arrived(n):
        @pl.when(row < 3)
        def _():
            halo(n, 0).wait_recv()

        @pl.when(row > 0)
        def _():
            halo(n, 1).wait_recv()

    def halo_sent(n):
        @pl.when(row > 0)
        def _():
            halo(n, 0).wait_send()

        @pl.when(row < 3)
        def _():
            halo(n, 1).wait_send()

    halo_start(0)
    halo_start(1)

    for at, edge in ((0, 0), (3, R + 1)):
        @pl.when(row == at)
        def _():
            zero = jnp.zeros((T, W, CH), BF16)
            xi[edge, :, :, CH:2 * CH] = zero
            ci[edge, :, :, CH:2 * CH] = zero
            sb[edge] = zero

    d_all = dec[...]
    sc[...] = jnp.sqrt((1.0 - d_all) * (1.0 + d_all))

    load_kout.wait()
    for i in range(3):
        for j in range(3):
            ft[(i * 3 + j) * CH:(i * 3 + j + 1) * CH, :] = kout[2 - i, 2 - j].T

    def widen(buf, r):
        def body(b, _):
            f0 = b * FB
            v = buf[r, pl.ds(f0, FB), :, CH:2 * CH].reshape(M, CH).astype(F32)
            buf[r, pl.ds(f0, FB), :, 0:CH] = from_left(v).astype(BF16).reshape(FB, W, CH)
            buf[r, pl.ds(f0, FB), :, 2 * CH:3 * CH] = from_right(v).astype(BF16).reshape(FB, W, CH)
            return 0

        lax.fori_loop(0, NB, body, 0)

    def conv(buf, weights, dst, first, stride, count):
        def body(n, _):
            h = first + (n // NB) * stride
            f0 = lax.rem(n, NB) * FB
            lhs = jnp.concatenate(
                [buf[h + i, pl.ds(f0, FB)].reshape(M, 3 * CH) for i in range(3)], axis=1
            )
            dst[h, pl.ds(f0, FB)] = jnp.dot(lhs, weights[...], preferred_element_type=F32).reshape(FB, W, CH)
            return 0

        lax.fori_loop(0, count * NB, body, 0)

    for n, load in enumerate(loads):
        load.wait()
    def widen_own(r, _):
        widen(xi, r)
        widen(ci, r)
        return 0

    lax.fori_loop(1, R + 1, widen_own, 0)
    load_kin.wait()
    conv(xi, kin, drv, 1, 1, 2)
    conv(ci, ft, adj, 1, 1, 2)
    halo_arrived(0)
    widen(xi, 0)
    widen(xi, R + 1)
    conv(xi, kin, drv, 0, 3, 2)

    UN = 4

    def decay_at(t):
        return dec[pl.ds(t, 1), :]

    def ends_forward(n, carry):
        state, prod = carry
        for u in range(UN):
            t = n * UN + u
            d = decay_at(t)
            state = d * state + sc[pl.ds(t, 1), :] * drv[:, t]
            prod = prod * d
        return state, prod

    def ends_backward(n, v):
        for u in range(UN):
            t = T - 1 - (n * UN + u)
            v = decay_at(t) * (adj[:, t] + v)
        return v

    zero_state = jnp.zeros((R, W, CH), F32)

    def broadcast_line(buf, way, axis, ssem, rsem, start):
        me = pos[axis]
        for d in (1, 2, 3):
            k = step(axis, d)
            if start:
                remote(buf.at[way, me], buf.at[way, me], ssem.at[way, d - 1], rsem.at[way, me], mate(axis, k)).start()
            else:
                copy = remote(buf.at[way, me], buf.at[way, k], ssem.at[way, d - 1], rsem.at[way, k], mate(axis, k))
                copy.wait()

    def fold(buf, way, axis):
        me = pos[axis]
        before = jnp.zeros((CELLS, CH), F32)
        before_decay = jnp.ones((1, CH), F32)
        total = before
        total_decay = before_decay
        for p in (range(4) if way == 0 else range(3, -1, -1)):
            e = buf[way, p, 0:CELLS]
            d = buf[way, p, CELLS:CELLS + 1]
            takes = (me > p) if way == 0 else (me < p)
            before = jnp.where(takes, d * before + e, before)
            before_decay = jnp.where(takes, before_decay * d, before_decay)
            total = d * total + e
            total_decay = total_decay * d
        return before, before_decay, total, total_decay

    def put(buf, way, axis, total, decay):
        me = pos[axis]
        buf[way, me, 0:CELLS] = total
        buf[way, me, CELLS:MSG] = jnp.broadcast_to(decay, (8, CH))

    y_mate = mate("y", (row // 2) * 2 + 1 - y_lo)

    def y_copy(way):
        return remote(ry.at[way, 0], ry.at[way, 1], ysend.at[way], yrecv.at[way], y_mate)

    def send_y(way):
        @pl.when(y_lo == way)
        def _():
            y_copy(way).start()

    def take_y(way, z_before, z_decay, x_before, x_decay):
        incoming[way] = x_decay * z_before + x_before

        @pl.when(y_lo == 1 - way)
        def _():
            y_copy(way).wait_recv()
            incoming[way] = x_decay * (z_decay * ry[way, 1] + z_before) + x_before

    end, decay = lax.fori_loop(0, T // UN, ends_forward, (zero_state, jnp.ones((1, CH), F32)))
    put(rx, 0, "x", end.reshape(CELLS, CH), decay)
    broadcast_line(rx, 0, "x", xsend, xrecv, True)

    halo_arrived(1)
    widen(ci, 0)
    widen(ci, R + 1)
    conv(ci, ft, adj, 0, 3, 2)
    lead = lax.fori_loop(0, T // UN, ends_backward, zero_state)
    put(rx, 1, "x", lead.reshape(CELLS, CH), decay)
    broadcast_line(rx, 1, "x", xsend, xrecv, True)

    broadcast_line(rx, 0, "x", xsend, xrecv, False)
    fx, fxd, total, total_decay = fold(rx, 0, "x")
    put(rz, 0, "z", total, total_decay)
    broadcast_line(rz, 0, "z", zsend, zrecv, True)

    broadcast_line(rx, 1, "x", xsend, xrecv, False)
    bx, bxd, total, total_decay = fold(rx, 1, "x")
    put(rz, 1, "z", total, total_decay)
    broadcast_line(rz, 1, "z", zsend, zrecv, True)

    broadcast_line(rz, 0, "z", zsend, zrecv, False)
    fz, fzd, total, _ = fold(rz, 0, "z")
    ry[0, 0] = total
    send_y(0)
    broadcast_line(rz, 1, "z", zsend, zrecv, False)
    bz, bzd, total, _ = fold(rz, 1, "z")
    ry[1, 0] = total
    send_y(1)

    take_y(0, fz, fzd, fx, fxd)

    def states(n, state):
        for u in range(UN):
            t = n * UN + u
            state = decay_at(t) * state + sc[pl.ds(t, 1), :] * drv[:, t]
            sb[1:R + 1, t] = state.astype(BF16)
        return state

    lax.fori_loop(0, T // UN, states, incoming[0].reshape(R, W, CH))
    halo_start(2)
    take_y(1, bz, bzd, bx, bxd)

    def grad_rows(field, other, other_at):
        def body(h, _):
            turned = field[h + other_at].reshape(T * W, CH).T
            for i in range(3):
                acc[i] += jnp.dot(turned, other[h + i].reshape(T * W, 3 * CH), preferred_element_type=F32)
            return 0
        return body

    def adjoints(n, v):
        for u in range(UN):
            t = T - 1 - (n * UN + u)
            a = adj[:, t] + v
            dcb[:, t] = (sc[pl.ds(t, 1), :] * a).astype(BF16)
            v = decay_at(t) * a
        return v

    def reduction(g):
        mine = pl.ds(0, 1)
        pair_copy = remote(psend.at[g], precv.at[g], psem.at[g], prem.at[g], pair)

        def begin():
            for i in range(3):
                for j in range(3):
                    n = i * 3 + j
                    if g == 0:
                        v = acc[2 - i, :, (2 - j) * CH:(3 - j) * CH]
                    else:
                        v = acc[i, :, j * CH:(j + 1) * CH].T
                    gbuf[0, n * 128:(n + 1) * 128, :] = v[0:128]
                    gbuf[1, n * 128:(n + 1) * 128, :] = v[128:256]
            psend[g] = gbuf[1 - core].astype(BF16)
            pair_copy.start()

        def first():
            pair_copy.wait()
            for q in range(3):
                for k in range(4):
                    at = q * 384 + k * 96
                    v = gbuf[core, at:at + 96, :] + precv[g, at:at + 96, :].astype(F32)
                    hbuf[q, k] = v
                    s1[g, q, k] = v.astype(BF16)
            for q in range(3):
                for d in (1, 2, 3):
                    k = step(ORDERS[q][0], d)
                    remote(s1.at[g, q, k], r1.at[g, q, d - 1], s1s.at[g, q, d - 1], s1r.at[g, q, d - 1],
                           mate(ORDERS[q][0], k)).start()

        def second():
            for q in range(3):
                axis = ORDERS[q][0]
                total = hbuf[q, pos[axis]]
                for d in (1, 2, 3):
                    k = step(axis, d)
                    remote(s1.at[g, q, k], r1.at[g, q, d - 1], s1s.at[g, q, d - 1], s1r.at[g, q, d - 1],
                           mate(axis, k)).wait()
                    total = total + r1[g, q, d - 1].astype(F32)
                for k in range(4):
                    c1[g, q, k] = total[48 * (k // 2):48 * (k // 2) + 48, 128 * (k % 2):128 * (k % 2) + 128]
                axis = ORDERS[q][1]
                for d in (1, 2, 3):
                    k = step(axis, d)
                    remote(c1.at[g, q, k], r2.at[g, q, d - 1], s2s.at[g, q, d - 1], s2r.at[g, q, d - 1],
                           mate(axis, k)).start()

        def third():
            for q in range(3):
                axis = ORDERS[q][1]
                total = c1[g, q, pos[axis]]
                for d in (1, 2, 3):
                    k = step(axis, d)
                    remote(c1.at[g, q, k], r2.at[g, q, d - 1], s2s.at[g, q, d - 1], s2r.at[g, q, d - 1],
                           mate(axis, k)).wait()
                    total = total + r2[g, q, d - 1]
                c2[g, q] = total
                axis = ORDERS[q][2]
                for d in (1, 2, 3):
                    remote(c2.at[g, q], r3.at[g, q, d - 1], s3s.at[g, q, d - 1], s3r.at[g, q, d - 1],
                           mate(axis, step(axis, d))).start()

        def spread_copy(q, d, arriving):
            axis = ORDERS[q][1]
            k1 = pos[ORDERS[q][0]]
            k2 = lax.rem(pos[axis] + 4 - d, 4) if arriving else pos[axis]
            return remote(agb.at[g, q, k1, k2], agb.at[g, q, k1, k2], a2s.at[g, q, d - 1], a2r.at[g, q, d - 1],
                          mate(axis, step(axis, d)))

        def wide_copy(q, d, arriving):
            axis = ORDERS[q][0]
            k1 = lax.rem(pos[axis] + 4 - d, 4) if arriving else pos[axis]
            return remote(agb.at[g, q, k1], agb.at[g, q, k1], a1s.at[g, q, d - 1], a1r.at[g, q, d - 1],
                          mate(axis, step(axis, d)))

        def hand_over(q, d):
            k1 = lax.rem(pos[ORDERS[q][0]] + 4 - d, 4)
            return remote(agb.at[g, q, k1], pgb.at[g, q, k1], pgs.at[g, q, d], pgr.at[g, q, d], pair)

        def fourth():
            for q in range(3):
                axis = ORDERS[q][2]
                for d in (1, 2, 3):
                    remote(c2.at[g, q], r3.at[g, q, d - 1], s3s.at[g, q, d - 1], s3r.at[g, q, d - 1],
                           mate(axis, step(axis, d))).wait()
                total = (c2[g, q] + r3[g, q, 1]) + (r3[g, q, 0] + r3[g, q, 2])
                agb[g, q, pos[ORDERS[q][0]], pos[ORDERS[q][1]]] = (total * grad_scale).astype(BF16)
                for d in (1, 2, 3):
                    spread_copy(q, d, False).start()

        def fifth():
            for q in range(3):
                for d in (1, 2, 3):
                    spread_copy(q, d, True).wait_recv()
                    spread_copy(q, d, False).wait_send()
                for d in (1, 2, 3):
                    wide_copy(q, d, False).start()
                hand_over(q, 0).start()

        def sixth():
            for d in (1, 2, 3):
                for q in range(3):
                    wide_copy(q, d, True).wait_recv()
                    wide_copy(q, d, False).wait_send()
                    hand_over(q, d).start()

        out = pltpu.make_async_copy(fb.at[g], (gout_hbm, gin_hbm)[g], gsem.at[g])

        def last():
            for q in range(3):
                for d in range(4):
                    hand_over(q, d).wait()
            for q in range(3):
                for k1 in range(4):
                    for k2 in range(4):
                        at = q * 384 + k1 * 96 + 48 * (k2 // 2)
                        lanes = slice(128 * (k2 % 2), 128 * (k2 % 2) + 128)
                        fb[g, core, at:at + 48, lanes] = agb[g, q, k1, k2]
                        fb[g, 1 - core, at:at + 48, lanes] = pgb[g, q, k1, k2]
            out.start()

        return [begin, first, second, third, fourth, fifth, sixth, last], out

    stages_out, done_out = reduction(0)
    stages_in, done_in = reduction(1)

    acc[...] = jnp.zeros_like(acc)
    lax.fori_loop(0, R, grad_rows(sb, ci, 1), 0)
    stages_out[0]()
    lax.fori_loop(0, T // UN, adjoints, incoming[1].reshape(R, W, CH))
    stages_out[1]()
    acc[...] = jnp.zeros_like(acc)
    body = grad_rows(dcb, xi, 0)
    lax.fori_loop(0, 2, body, 0)
    stages_out[2]()
    lax.fori_loop(2, 4, body, 0)
    stages_in[0]()
    stages_out[3]()
    halo_arrived(2)

    def mix(h):
        def block(b, _):
            f0 = b * FB
            lhs = jnp.concatenate([sb[h + i, pl.ds(f0, FB)].reshape(M, CH) for i in range(3)], axis=1)
            parts = []
            for j in range(3):
                weights = jnp.concatenate([kout[i, j] for i in range(3)], axis=0)
                parts.append(jnp.dot(lhs, weights, preferred_element_type=F32))
            x = xi[h + 1, pl.ds(f0, FB), :, CH:2 * CH].reshape(M, CH).astype(F32)
            y = from_left(parts[0]) + parts[1] + from_right(parts[2]) + skip[...] * x
            ob[h, pl.ds(f0, FB)] = y.astype(BF16).reshape(FB, W, CH)
            return 0

        lax.fori_loop(0, NB, block, 0)
        store = pltpu.make_async_copy(ob.at[h], out_hbm.at[:, h], osem.at[h])
        store.start()
        return store

    stages_in[1]()
    stores = [mix(0)]
    stages_out[4]()
    stages_in[2]()
    stores.append(mix(1))
    stages_out[5]()
    stages_in[3]()
    stores.append(mix(2))
    stages_out[6]()
    stages_in[4]()
    stores.append(mix(3))
    stages_in[5]()
    stages_out[7]()
    stages_in[6]()
    stages_in[7]()

    for n in range(3):
        halo_sent(n)
    for way in range(2):
        @pl.when(y_lo == way)
        def _():
            y_copy(way).wait_send()
    for store in stores:
        store.wait()
    done_out.wait()
    done_in.wait()


def per_device(inputs, decays, in_kernel, out_kernel, skip, cotangent):
    cells_all = T * lax.axis_size("tm") * R * lax.axis_size("row") * W
    grad_scale = 1.0 / math.sqrt(cells_all)
    anywhere = pl.BlockSpec(memory_space=pl.ANY)
    vmem = pl.BlockSpec(memory_space=pltpu.VMEM)
    dma = pltpu.SemaphoreType.DMA
    V = pltpu.VMEM
    half = jax.ShapeDtypeStruct((2, HALF, CH), BF16)
    outputs, in_grad, out_grad = pl.pallas_call(
        functools.partial(kernel, grad_scale),
        out_shape=(jax.ShapeDtypeStruct((T, R, W, CH), BF16), half, half),
        in_specs=[anywhere, vmem, anywhere, anywhere, vmem, anywhere],
        out_specs=(anywhere, anywhere, anywhere),
        scratch_shapes=[
            V((R + 2, T, W, 3 * CH), BF16),
            V((R + 2, T, W, 3 * CH), BF16),
            V((9 * CH, CH), BF16),
            V((3, 3, CH, CH), BF16),
            V((9 * CH, CH), BF16),
            V((R, T, W, CH), F32),
            V((R, T, W, CH), F32),
            V((R + 2, T, W, CH), BF16),
            V((R, T, W, CH), BF16),
            V((R, T, W, CH), BF16),
            V((T, CH), F32),
            V((2, 4, MSG, CH), F32),
            V((2, 4, MSG, CH), F32),
            V((2, 2, CELLS, CH), F32),
            V((2, CELLS, CH), F32),
            V((3, CH, 3 * CH), F32),
            V((2, HALF, CH), F32),
            V((2, HALF, CH), BF16),
            V((2, HALF, CH), BF16),
            V((3, 4, 96, CH), F32),
            V((2, 3, 4, 96, CH), BF16),
            V((2, 3, 3, 96, CH), BF16),
            V((2, 3, 4, 48, 128), F32),
            V((2, 3, 3, 48, 128), F32),
            V((2, 3, 48, 128), F32),
            V((2, 3, 3, 48, 128), F32),
            V((2, 3, 4, 4, 48, 128), BF16),
            V((2, 3, 4, 4, 48, 128), BF16),
            V((2, 2, HALF, CH), BF16),
            dma((2, R)), dma((2,)), dma((R,)), dma((2,)),
            dma((3, 2)), dma((3, 2)),
            dma((2, 3)), dma((2, 4)), dma((2, 3)), dma((2, 4)), dma((2,)), dma((2,)),
            dma((2,)), dma((2,)),
            dma((2, 3, 3)), dma((2, 3, 3)), dma((2, 3, 3)), dma((2, 3, 3)), dma((2, 3, 3)), dma((2, 3, 3)),
            dma((2, 3, 3)), dma((2, 3, 3)), dma((2, 3, 3)), dma((2, 3, 3)),
            dma((2, 3, 4)), dma((2, 3, 4)),
        ],
        compiler_params=pltpu.CompilerParams(
            collective_id=0, has_side_effects=True, vmem_limit_bytes=62 * 1024 * 1024
        ),
    )(
        inputs.reshape(T, R, W, CH), decays, in_kernel.reshape(9 * CH, CH), out_kernel,
        skip.reshape(1, CH), cotangent.reshape(T, R, W, CH),
    )

    def whole(halves):
        return halves.reshape(2, 9, 128, CH).transpose(1, 0, 2, 3).reshape(3, 3, CH, CH).astype(F32)

    return outputs.reshape(inputs.shape), whole(in_grad), whole(out_grad)


def solution(mesh):
    return jax.shard_map(
        per_device,
        mesh=mesh,
        in_specs=(
            P(None, "tm", "row", None, None),
            P("tm", None),
            P(),
            P(),
            P(),
            P(None, "tm", "row", None, None),
        ),
        out_specs=(P(None, "tm", "row", None, None), P(), P()),
        check_vma=False,
    )
```

time: 1430 us -> 97.2 us (0.07); the launches traced: 1410 us -> 96.9 us
  waiting for transfers between devices: 448 us -> 0 us
  local copies, waits for them, and re-layouts: 449 us -> 5.47 us
  starting transfers between devices: 361 us -> 0 us
  Pallas kernels: 0 us -> 89 us
  matrix products: 69.3 us -> 0 us
  other arithmetic: 62.2 us -> 1.78 us
  between operations: 15.5 us -> 0.67 us
    ppermute x68 -> x0, starting transfers between devices: 361 us -> none  [the longest x62 273 us: passed_along(): return lax.ppermute(shard, axis, pairs)]
    pad x20 -> x0, local copies, waits for them, and re-layouts: 269 us -> none  [local_recurrence(): lax.associative_scan(linear_combine, (jnp.broadcast_to(factors, terms.sha...]
    psum x1 -> x0, waiting for transfers between devices: 225 us -> none  [per_device(): in_grad, out_grad = lax.psum((in_grad, out_grad), ('tm', 'row'))]
    ppermute x68 -> x0, waiting for transfers between devices: 223 us -> none  [the longest x62 223 us: passed_along(): return lax.ppermute(shard, axis, pairs)]
    slice x78 -> x0, local copies, waits for them, and re-layouts: 148 us -> none  [the longest x71 144 us: local_recurrence(): lax.associative_scan(linear_combine, (jnp.broadcast_to(factors, terms.sha...]
    pallas_call x0 -> x1, Pallas kernels: none -> 89 us  [per_device(): pl.pallas_call(functools.partial(kernel, grad_scale), out_shape=(jax.Shap...]
    dot_general x18 -> x0, matrix products: 46.6 us -> none  [tap_grads(): lax.dot_general(window, cotan_flat, (((0, 1, 2), (0, 1, 2)), ((), ())), p...]
    add x91 -> x0, other arithmetic: 34.2 us -> none  [the longest x11 18.2 us: local_recurrence(): lax.associative_scan(linear_combine, (jnp.broadcast_to(factors, terms.sha...]
  transfers between devices with their start and end apart: 69 -> 0, of which waited for: 63 -> 0; matrix products, arithmetic and copies ran while one was open for 10% -> 0% of each run, Pallas kernels for 0% -> 0%
where the time goes in v1:
time: 97.2 us; the launch traced here: 96.9 us
  Pallas kernels  89 us (92%)
  local copies, waits for them, and re-layouts  5.47 us (6%)
  other arithmetic  1.78 us (2%)
    pallas_call x1, Pallas kernels, per_device(): pl.pallas_call(functools.partial(kernel, grad_scale), out_shape=(jax.Shap...  89 us
    convert_element_type x2, local copies, waits for them, and re-layouts, whole(): halves.reshape(2, 9, 128, CH).transpose(1, 0, 2, 3).reshape(3, 3, CH, CH)  3.12 us
    unnamed x5, local copies, waits for them, and re-layouts  2.35 us

profile of v1, /device:TPU:1, one launch (start us, length us, event | category | flops | bytes accessed | tf_op | source)
XLA Modules:
  0.0 96.9 jit_solution(12711686548194900809)
XLA Ops:
  0.6 89.0 %shard_map.85 = (bf16[64,4,16,256]{3,2,1,0:T(8,128)(2,1)}, bf16[2,1152,256]{2,1,0:T(8,128)(2,1)}, bf16[2,1152,256]{2,1,0:T(8,128)(2,1)}) custom-call(bf16[64,4,16,256]{3,2,1,0:T(8,128)(2,1)} %bitcast.17, f32[64,256]{1,0:T(8,128)} %dec.1, bf16[2304,256]{1,0:T(8,128)(2,1)} %bitcast.22, bf16[3,3,256,256]{3,2,1,0:T(8,128)(2,1)} %kout_hbm.1, f32[1,256]{1,0:T(1,128)} %bitcast.23, ...), custom_call_target="tpu_custom_call" | custom-call | tf_op jit(solution)/shard_map/pallas_call | solution.py:529
  89.6 1.5 %convert_bitcast_fusion.1 = f32[9,2,128,256]{3,2,0,1:T(8,128)S(1)} fusion(bf16[2,9,128,256]{3,2,1,0:T(8,128)(2,1)} %bitcast.21), kind=kLoop, calls=%fused_computation.1 | loop fusion | flops 589824 | bytes 3538944 | tf_op jit(solution)/shard_map/convert_element_type | solution.py:581
  91.1 0.0 copy-start.1
  91.2 1.6 %copy.9 = f32[9,2,128,256]{3,2,1,0:T(8,128)} copy(f32[9,2,128,256]{3,2,0,1:T(8,128)S(1)} %convert_bitcast_fusion.1) | data formatting | bytes 4718592 | tf_op jit(solution)/shard_map/convert_element_type | solution.py:581
  92.7 0.2 copy-done.1
  92.9 0.3 convert_bitcast_fusion
  93.1 0.0 copy-start
  93.1 1.6 %copy.10 = f32[9,2,128,256]{3,2,1,0:T(8,128)} copy(f32[9,2,128,256]{3,2,0,1:T(8,128)S(1)} %convert_bitcast_fusion) | data formatting | bytes 4718592 | tf_op jit(solution)/shard_map/convert_element_type | solution.py:581
  94.7 0.9 copy-done
  95.6 1.3 %copy.12 = bf16[1,64,4,16,256]{4,3,2,1,0:T(8,128)(2,1)} copy(bf16[1,64,4,16,256]{4,3,2,1,0:T(8,128)(2,1)S(1)} %bitcast.19) | data formatting | bytes 4194304
Async XLA Ops:
  91.1 1.7 %copy-start.1 = (bf16[2,1152,256]{2,1,0:T(8,128)(2,1)S(1)}, bf16[2,1152,256]{2,1,0:T(8,128)(2,1)}, u32[]{:S(2)}) copy-start(bf16[2,1152,256]{2,1,0:T(8,128)(2,1)} %get-tuple-element.8) | copy-start | bytes 3538948
  93.1 2.4 %copy-start = (bf16[64,4,16,256]{3,2,1,0:T(8,128)(2,1)S(1)}, bf16[64,4,16,256]{3,2,1,0:T(8,128)(2,1)}, u32[]{:S(2)}) copy-start(bf16[64,4,16,256]{3,2,1,0:T(8,128)(2,1)} %get-tuple-element.6) | copy-start | bytes 6291460

commit v2 on v1

v2 whole, which is shorter than its diff:
```python
import functools
import math

import jax
import jax.numpy as jnp
from jax import lax
from jax.experimental import pallas as pl
from jax.experimental.pallas import tpu as pltpu
from jax.sharding import PartitionSpec as P

MESH = pl.DeviceIdType.MESH
F32 = jnp.float32
BF16 = jnp.bfloat16

T = 64
R = 4
W = 16
CH = 256
FB = 32
NB = T // FB
M = FB * W
CELLS = R * W
MSG = CELLS + 8
LINE = 4
CHUNK = (48, 128)
ORDERS = (("x", "z", "y"), ("z", "y", "x"), ("y", "x", "z"))


def column(rows):
    return lax.broadcasted_iota(jnp.int32, (rows, CH), 0) & (W - 1)


def from_left(v):
    return jnp.where(column(v.shape[0]) == 0, 0.0, pltpu.roll(v, 1, 0))


def from_right(v):
    return jnp.where(column(v.shape[0]) == W - 1, 0.0, pltpu.roll(v, v.shape[0] - 1, 0))


def kernel(
    grad_scale,
    x_hbm, dec, kin_hbm, kout_hbm, skip, cot_hbm,
    out_hbm, gin_hbm, gout_hbm,
    xi, ci, kin, kout, ft, drv, adj, sb, dcb, ob, sc,
    rx, rz, ry, incoming,
    turned, acc, psend, precv, h1, h2, own, s1, r1, c1, r2, c2, r3, agb, pgb, fb,
    lsem, wsem, osem, gsem,
    hsend, hrecv, xsend, xrecv, zsend, zrecv, ysend, yrecv,
    psem, prem, s1s, s1r, s2s, s2r, s3s, s3r, a2s, a2r, a1s, a1r, pgs, pgr,
):
    tm = lax.axis_index("tm")
    row = lax.axis_index("row")
    core = lax.rem(row, 2)
    y_lo = tm // 16
    pos = {"x": lax.rem(tm, 4), "z": lax.rem(tm // 4, 4), "y": (row // 2) * 2 + y_lo}

    def mate(axis, k):
        if axis == "x":
            return ((tm // 4) * 4 + k, row)
        if axis == "z":
            return (y_lo * 16 + k * 4 + lax.rem(tm, 4), row)
        return (lax.rem(k, 2) * 16 + lax.rem(tm, 16), (k // 2) * 2 + core)

    def mates(axis):
        return [mate(axis, lax.rem(pos[axis] + d, LINE)) for d in (1, 2, 3)]

    pair = (tm, row + 1 - 2 * core)
    up = (tm, row - 1)
    down = (tm, row + 1)

    def remote(src, dst, ssem, rsem, device):
        return pltpu.make_async_remote_copy(
            src_ref=src, dst_ref=dst, send_sem=ssem, recv_sem=rsem,
            device_id=device, device_id_type=MESH,
        )

    barrier = pltpu.get_barrier_semaphore()

    def greet(device):
        pl.semaphore_signal(barrier, inc=1, device_id=device, device_id_type=MESH)

    @pl.when(row == 1)
    def _():
        greet(down)

    @pl.when(row == 2)
    def _():
        greet(up)

    greet(pair)
    for axis in ("y", "x", "z"):
        for device in mates(axis):
            greet(device)

    mid = pl.ds(CH, CH)
    loads = [
        [
            pltpu.make_async_copy(hbm.at[:, r], buf.at[r + 1, :, :, mid], lsem.at[n, r])
            for r in range(R)
        ]
        for n, (hbm, buf) in enumerate(((x_hbm, xi), (cot_hbm, ci)))
    ]
    load_kin = pltpu.make_async_copy(kin_hbm, kin, wsem.at[0])
    load_kout = pltpu.make_async_copy(kout_hbm, kout, wsem.at[1])
    for load in loads[0]:
        load.start()
    load_kin.start()
    load_kout.start()
    for load in loads[1]:
        load.start()

    for at, edge in ((0, 0), (3, R + 1)):
        @pl.when(row == at)
        def _():
            zero = jnp.zeros((T, W, CH), BF16)
            xi[edge, :, :, CH:2 * CH] = zero
            ci[edge, :, :, CH:2 * CH] = zero
            sb[edge] = zero

    d_all = dec[...]
    sc[...] = jnp.sqrt((1.0 - d_all) * (1.0 + d_all))

    @pl.when((row == 1) | (row == 2))
    def _():
        pl.semaphore_wait(barrier, 11)

    @pl.when((row == 0) | (row == 3))
    def _():
        pl.semaphore_wait(barrier, 10)

    def halo(n, way):
        if n == 2:
            src = sb.at[1] if way == 0 else sb.at[R]
            dst = sb.at[R + 1] if way == 0 else sb.at[0]
        else:
            hbm, buf = ((x_hbm, xi), (cot_hbm, ci))[n]
            src = hbm.at[:, 0] if way == 0 else hbm.at[:, R - 1]
            dst = buf.at[R + 1, :, :, mid] if way == 0 else buf.at[0, :, :, mid]
        return remote(src, dst, hsend.at[n, way], hrecv.at[n, way], up if way == 0 else down)

    def halo_start(n):
        @pl.when(row > 0)
        def _():
            halo(n, 0).start()

        @pl.when(row < 3)
        def _():
            halo(n, 1).start()

    def halo_arrived(n):
        @pl.when(row < 3)
        def _():
            halo(n, 0).wait_recv()

        @pl.when(row > 0)
        def _():
            halo(n, 1).wait_recv()

    def halo_sent(n):
        @pl.when(row > 0)
        def _():
            halo(n, 0).wait_send()

        @pl.when(row < 3)
        def _():
            halo(n, 1).wait_send()

    halo_start(0)
    halo_start(1)

    def widen(buf, r):
        def body(b, _):
            f0 = b * FB
            v = buf[r, pl.ds(f0, FB), :, CH:2 * CH].reshape(M, CH).astype(F32)
            buf[r, pl.ds(f0, FB), :, 0:CH] = from_left(v).astype(BF16).reshape(FB, W, CH)
            buf[r, pl.ds(f0, FB), :, 2 * CH:3 * CH] = from_right(v).astype(BF16).reshape(FB, W, CH)
            return 0

        lax.fori_loop(0, NB, body, 0)

    def conv(buf, weights, dst, first, stride, count):
        def body(n, _):
            h = first + (n // NB) * stride
            f0 = lax.rem(n, NB) * FB
            lhs = jnp.concatenate(
                [buf[h + i, pl.ds(f0, FB)].reshape(M, 3 * CH) for i in range(3)], axis=1
            )
            dst[h, pl.ds(f0, FB)] = jnp.dot(lhs, weights[...], preferred_element_type=F32).reshape(FB, W, CH)
            return 0

        lax.fori_loop(0, count * NB, body, 0)

    def turn_kernel():
        for i in range(3):
            for j in range(3):
                ft[(i * 3 + j) * CH:(i * 3 + j + 1) * CH, :] = kout[2 - i, 2 - j].T

    def widen_own(buf):
        def body(r, _):
            widen(buf, r)
            return 0

        lax.fori_loop(1, R + 1, body, 0)

    UN = 4

    def decay_at(t):
        return dec[pl.ds(t, 1), :]

    def ends_forward(n, carry):
        state, prod = carry
        for u in range(UN):
            t = n * UN + u
            d = decay_at(t)
            state = d * state + sc[pl.ds(t, 1), :] * drv[:, t]
            prod = prod * d
        return state, prod

    def ends_backward(n, v):
        for u in range(UN):
            t = T - 1 - (n * UN + u)
            v = decay_at(t) * (adj[:, t] + v)
        return v

    zero_state = jnp.zeros((R, W, CH), F32)

    def line(buf, way, axis, ssem, rsem, start):
        me = pos[axis]
        for d in (1, 2, 3):
            k = lax.rem(me + d, LINE)
            if start:
                remote(buf.at[way, me], buf.at[way, me], ssem.at[way, d - 1], rsem.at[way, me], mate(axis, k)).start()
            else:
                remote(buf.at[way, me], buf.at[way, k], ssem.at[way, d - 1], rsem.at[way, k], mate(axis, k)).wait()

    def fold(buf, way, me):
        before = jnp.zeros((CELLS, CH), F32)
        before_decay = jnp.ones((1, CH), F32)
        total = before
        total_decay = before_decay
        for p in (range(4) if way == 0 else range(3, -1, -1)):
            e, d = buf[way, p, 0:CELLS], buf[way, p, CELLS:CELLS + 1]
            takes = (me > p) if way == 0 else (me < p)
            before = jnp.where(takes, d * before + e, before)
            before_decay = jnp.where(takes, before_decay * d, before_decay)
            total = d * total + e
            total_decay = total_decay * d
        return before, before_decay, total, total_decay

    def put(buf, way, axis, total, decay):
        buf[way, pos[axis], 0:CELLS] = total
        buf[way, pos[axis], CELLS:MSG] = jnp.broadcast_to(decay, (8, CH))

    def y_copy(way):
        return remote(ry.at[way, 0], ry.at[way, 1], ysend.at[way], yrecv.at[way],
                      mate("y", (row // 2) * 2 + 1 - y_lo))

    def x_start(way, total, decay):
        put(rx, way, "x", total, decay)
        line(rx, way, "x", xsend, xrecv, True)

    def x_to_z(way):
        line(rx, way, "x", xsend, xrecv, False)
        before, before_decay, total, total_decay = fold(rx, way, pos["x"])
        put(rz, way, "z", total, total_decay)
        line(rz, way, "z", zsend, zrecv, True)
        return before, before_decay

    def z_to_y(way):
        line(rz, way, "z", zsend, zrecv, False)
        before, before_decay, total, _ = fold(rz, way, pos["z"])
        ry[way, 0] = total

        @pl.when(y_lo == way)
        def _():
            y_copy(way).start()

        return before, before_decay

    def from_y(way, z_side, x_side):
        z_before, z_decay = z_side
        x_before, x_decay = x_side
        incoming[way] = x_decay * z_before + x_before

        @pl.when(y_lo == 1 - way)
        def _():
            y_copy(way).wait_recv()
            incoming[way] = x_decay * (z_decay * ry[way, 1] + z_before) + x_before

    def states(n, state):
        for u in range(UN):
            t = n * UN + u
            state = decay_at(t) * state + sc[pl.ds(t, 1), :] * drv[:, t]
            sb[1:R + 1, t] = state.astype(BF16)
        return state

    for load in loads[0]:
        load.wait()
    widen_own(xi)
    load_kin.wait()
    conv(xi, kin, drv, 1, 1, 2)
    halo_arrived(0)
    widen(xi, 0)
    widen(xi, R + 1)
    conv(xi, kin, drv, 0, 3, 2)
    end, decay = lax.fori_loop(0, T // UN, ends_forward, (zero_state, jnp.ones((1, CH), F32)))
    x_start(0, end.reshape(CELLS, CH), decay)

    load_kout.wait()
    turn_kernel()
    for load in loads[1]:
        load.wait()
    widen_own(ci)
    conv(ci, ft, adj, 1, 1, 1)
    fx = x_to_z(0)
    conv(ci, ft, adj, 2, 1, 1)
    halo_arrived(1)
    widen(ci, 0)
    widen(ci, R + 1)
    conv(ci, ft, adj, 0, 1, 1)
    fz = z_to_y(0)
    conv(ci, ft, adj, 3, 1, 1)
    lead = lax.fori_loop(0, T // UN, ends_backward, zero_state)
    x_start(1, lead.reshape(CELLS, CH), decay)
    from_y(0, fz, fx)
    lax.fori_loop(0, T // UN, states, incoming[0].reshape(R, W, CH))
    halo_start(2)

    def turn(field, at):
        def body(h, _):
            turned[h] = field[h + at].reshape(T * W, CH).T
            return 0

        lax.fori_loop(0, R, body, 0)

    def row_tap(g, other, i):
        acc[g, i] = jnp.dot(turned[0], other[i].reshape(T * W, 3 * CH), preferred_element_type=F32)

        def body(h, _):
            acc[g, i] += jnp.dot(turned[h], other[h + i].reshape(T * W, 3 * CH), preferred_element_type=F32)
            return 0

        lax.fori_loop(1, R, body, 0)

    def adjoints(n, v):
        for u in range(UN):
            t = T - 1 - (n * UN + u)
            a = adj[:, t] + v
            dcb[:, t] = (sc[pl.ds(t, 1), :] * a).astype(BF16)
            v = decay_at(t) * a
        return v

    def part(g, q):
        pair_copy = remote(psend.at[g, q], precv.at[g, q], psem.at[g, q], prem.at[g, q], pair)

        def half(t, which):
            if g == 0:
                return acc[g, 2 - q, pl.ds(pl.multiple_of(which * 128, 128), 128), (2 - t) * CH:(3 - t) * CH]
            return acc[g, q, :, pl.ds(pl.multiple_of(t * CH + which * 128, 128), 128)].T

        def begin():
            for t in range(3):
                psend[g, q, t * 128:(t + 1) * 128] = half(t, 1 - core).astype(BF16)
            pair_copy.start()

        axis_1, axis_2, axis_3 = ORDERS[q]
        me_1, me_2 = pos[axis_1], pos[axis_2]

        def scatter():
            for t in range(3):
                h1[t * 128:(t + 1) * 128] = half(t, core)
            pair_copy.wait()
            for k in range(LINE):
                at = 96 * k
                v = h1[at:at + 96] + precv[g, q, at:at + 96].astype(F32)
                h2[k] = v
                s1[g, q, k] = v.astype(BF16)
            own[g, q] = h2[me_1]
            for d in (1, 2, 3):
                k = lax.rem(me_1 + d, LINE)
                remote(s1.at[g, q, k], r1.at[g, q, d - 1], s1s.at[g, q], s1r.at[g, q], mate(axis_1, k)).start()

        def second():
            remote(r1.at[g, q], r1.at[g, q], s1s.at[g, q], s1r.at[g, q], pair).wait()
            total = own[g, q]
            for d in range(3):
                total = total + r1[g, q, d].astype(F32)
            for k in range(LINE):
                c1[g, q, k] = total[48 * (k // 2):48 * (k // 2) + 48, 128 * (k % 2):128 * (k % 2) + 128]
            for d in (1, 2, 3):
                k = lax.rem(me_2 + d, LINE)
                remote(c1.at[g, q, k], r2.at[g, q, d - 1], s2s.at[g, q], s2r.at[g, q], mate(axis_2, k)).start()

        def cross():
            remote(r2.at[g, q], r2.at[g, q], s2s.at[g, q], s2r.at[g, q], pair).wait()
            c2[g, q] = c1[g, q, me_2] + r2[g, q, 0] + r2[g, q, 1] + r2[g, q, 2]
            for device, n in zip(mates(axis_3), range(3)):
                remote(c2.at[g, q], r3.at[g, q, n], s3s.at[g, q], s3r.at[g, q], device).start()

        def gather():
            remote(r3.at[g, q], r3.at[g, q], s3s.at[g, q], s3r.at[g, q], pair).wait()
            total = (c2[g, q] + r3[g, q, 1]) + (r3[g, q, 0] + r3[g, q, 2])
            mine = agb.at[g, q, me_1, me_2]
            mine[...] = (total * grad_scale).astype(BF16)
            for device in mates(axis_2):
                remote(mine, mine, a2s.at[g, q], a2r.at[g, q], device).start()

        def widen_out():
            three = agb.at[g, q, 0, pl.ds(0, 3)]
            remote(three, three, a2s.at[g, q], a2r.at[g, q], pair).wait()
            mine = agb.at[g, q, me_1]
            for device in mates(axis_1):
                remote(mine, mine, a1s.at[g, q], a1r.at[g, q], device).start()

        hand_over = remote(agb.at[g, q], pgb.at[g, q], pgs.at[g, q], pgr.at[g, q], pair)

        def share():
            three = agb.at[g, q, pl.ds(0, 3)]
            remote(three, three, a1s.at[g, q], a1r.at[g, q], pair).wait()
            hand_over.start()

        def unpack(buf, which):
            for k in range(LINE * LINE):
                at, lane = 48 * (k // 2), 128 * (k % 2)
                while at < 48 * (k // 2) + 48:
                    n = min(48 * (k // 2) + 48, (at // 128 + 1) * 128) - at
                    first = at - 48 * (k // 2)
                    fb[g, 3 * q + at // 128, which, at % 128:at % 128 + n, lane:lane + 128] = buf[g, q, k // LINE, k % LINE, first:first + n]
                    at += n

        def last():
            unpack(agb, core)
            hand_over.wait()
            unpack(pgb, 1 - core)
            out(g, q).start()

        return [begin, scatter, second, cross, gather, widen_out, share, last]

    def out(g, q):
        return pltpu.make_async_copy(
            fb.at[g, 3 * q:3 * q + 3], (gout_hbm, gin_hbm)[g].at[3 * q:3 * q + 3], gsem.at[g, q]
        )

    ro = [part(0, q) for q in range(3)]
    ri = [part(1, q) for q in range(3)]

    def run(*steps):
        for stages, n in steps:
            stages[n]()

    def mix(h):
        def block(b, _):
            f0 = b * FB
            lhs = jnp.concatenate([sb[h + i, pl.ds(f0, FB)].reshape(M, CH) for i in range(3)], axis=1)
            parts = []
            for j in range(3):
                weights = jnp.concatenate([kout[i, j] for i in range(3)], axis=0)
                parts.append(jnp.dot(lhs, weights, preferred_element_type=F32))
            x = xi[h + 1, pl.ds(f0, FB), :, CH:2 * CH].reshape(M, CH).astype(F32)
            y = from_left(parts[0]) + parts[1] + from_right(parts[2]) + skip[...] * x
            ob[h, pl.ds(f0, FB)] = y.astype(BF16).reshape(FB, W, CH)
            return 0

        lax.fori_loop(0, NB, block, 0)
        store = pltpu.make_async_copy(ob.at[h], out_hbm.at[:, h], osem.at[h])
        store.start()
        return store

    turn(sb, 1)
    row_tap(0, ci, 2)
    run((ro[0], 0))
    bx = x_to_z(1)
    row_tap(0, ci, 1)
    run((ro[1], 0), (ro[0], 1))
    row_tap(0, ci, 0)
    run((ro[2], 0), (ro[1], 1))
    bz = z_to_y(1)
    stores = [mix(1)]
    run((ro[2], 1), (ro[0], 2))
    from_y(1, bz, bx)
    lax.fori_loop(0, T // UN, adjoints, incoming[1].reshape(R, W, CH))
    turn(dcb, 0)
    row_tap(1, xi, 0)
    run((ri[0], 0), (ro[1], 2), (ro[2], 2), (ro[0], 3))
    row_tap(1, xi, 1)
    run((ri[1], 0), (ri[0], 1), (ro[1], 3), (ro[2], 3))
    row_tap(1, xi, 2)
    run((ri[2], 0), (ri[1], 1), (ro[0], 4), (ri[2], 1), (ri[0], 2), (ro[1], 4), (ro[2], 4))
    stores.append(mix(2))
    run((ri[1], 2), (ri[2], 2), (ri[0], 3), (ro[0], 5), (ro[1], 5), (ro[2], 5))
    halo_arrived(2)
    stores.append(mix(0))
    run((ri[1], 3), (ri[2], 3), (ri[0], 4), (ro[0], 6), (ro[1], 6), (ro[2], 6))
    stores.append(mix(3))
    run((ri[1], 4), (ri[2], 4), (ri[0], 5), (ro[0], 7), (ro[1], 7), (ro[2], 7))
    run((ri[1], 5), (ri[2], 5), (ri[0], 6))
    run((ri[1], 6), (ri[2], 6), (ri[0], 7), (ri[1], 7), (ri[2], 7))

    for n in range(3):
        halo_sent(n)
    for way in range(2):
        @pl.when(y_lo == way)
        def _():
            y_copy(way).wait_send()

    for store in stores:
        store.wait()
    for g in range(2):
        for q in range(3):
            out(g, q).wait()


def per_device(inputs, decays, in_kernel, out_kernel, skip, cotangent):
    cells_all = T * lax.axis_size("tm") * R * lax.axis_size("row") * W
    grad_scale = 1.0 / math.sqrt(cells_all)
    anywhere = pl.BlockSpec(memory_space=pl.ANY)
    vmem = pl.BlockSpec(memory_space=pltpu.VMEM)
    dma = pltpu.SemaphoreType.DMA
    V = pltpu.VMEM
    grad = jax.ShapeDtypeStruct((9, 2, 128, CH), BF16)
    outputs, in_grad, out_grad = pl.pallas_call(
        functools.partial(kernel, grad_scale),
        out_shape=(jax.ShapeDtypeStruct((T, R, W, CH), BF16), grad, grad),
        in_specs=[anywhere, vmem, anywhere, anywhere, vmem, anywhere],
        out_specs=(anywhere, anywhere, anywhere),
        scratch_shapes=[
            V((R + 2, T, W, 3 * CH), BF16),
            V((R + 2, T, W, 3 * CH), BF16),
            V((9 * CH, CH), BF16),
            V((3, 3, CH, CH), BF16),
            V((9 * CH, CH), BF16),
            V((R, T, W, CH), F32),
            V((R, T, W, CH), F32),
            V((R + 2, T, W, CH), BF16),
            V((R, T, W, CH), BF16),
            V((R, T, W, CH), BF16),
            V((T, CH), F32),
            V((2, 4, MSG, CH), F32),
            V((2, 4, MSG, CH), F32),
            V((2, 2, CELLS, CH), F32),
            V((2, CELLS, CH), F32),
            V((R, CH, T * W), BF16),
            V((2, 3, CH, 3 * CH), F32),
            V((2, 3, 384, CH), BF16),
            V((2, 3, 384, CH), BF16),
            V((384, CH), F32),
            V((LINE, 96, CH), F32),
            V((2, 3, 96, CH), F32),
            V((2, 3, LINE, 96, CH), BF16),
            V((2, 3, 3, 96, CH), BF16),
            V((2, 3, LINE) + CHUNK, F32),
            V((2, 3, 3) + CHUNK, F32),
            V((2, 3) + CHUNK, F32),
            V((2, 3, 3) + CHUNK, F32),
            V((2, 3, LINE, LINE) + CHUNK, BF16),
            V((2, 3, LINE, LINE) + CHUNK, BF16),
            V((2, 9, 2, 128, CH), BF16),
            dma((2, R)), dma((2,)), dma((R,)), dma((2, 3)),
            dma((3, 2)), dma((3, 2)),
            dma((2, 3)), dma((2, 4)), dma((2, 3)), dma((2, 4)), dma((2,)), dma((2,)),
            dma((2, 3)), dma((2, 3)), dma((2, 3)), dma((2, 3)), dma((2, 3)), dma((2, 3)), dma((2, 3)),
            dma((2, 3)), dma((2, 3)), dma((2, 3)), dma((2, 3)), dma((2, 3)), dma((2, 3)), dma((2, 3)),
        ],
        compiler_params=pltpu.CompilerParams(
            collective_id=0, has_side_effects=True, vmem_limit_bytes=62 * 1024 * 1024
        ),
    )(
        inputs.reshape(T, R, W, CH), decays, in_kernel.reshape(9 * CH, CH), out_kernel,
        skip.reshape(1, CH), cotangent.reshape(T, R, W, CH),
    )

    def whole(grad):
        return grad.reshape(3, 3, CH, CH).astype(F32)

    return outputs.reshape(inputs.shape), whole(in_grad), whole(out_grad)


def solution(mesh):
    return jax.shard_map(
        per_device,
        mesh=mesh,
        in_specs=(
            P(None, "tm", "row", None, None),
            P("tm", None),
            P(),
            P(),
            P(),
            P(None, "tm", "row", None, None),
        ),
        out_specs=(P(None, "tm", "row", None, None), P(), P()),
        check_vma=False,
    )
```

time: 97.2 us -> 91.1 us (0.937)
  Pallas kernels: 89 us -> 83.5 us
  local copies, waits for them, and re-layouts: 5.47 us -> 2.14 us
  other arithmetic: 1.78 us -> 4.62 us
    pallas_call x1, Pallas kernels: 89 us -> 83.5 us  [per_device(): pl.pallas_call(functools.partial(kernel, grad_scale), out_shape=(jax.Shap...]
    convert_element_type x2 -> x0, local copies, waits for them, and re-layouts: 3.12 us -> none  [whole(): halves.reshape(2, 9, 128, CH).transpose(1, 0, 2, 3).reshape(3, 3, CH, CH)]
    convert_element_type x2, other arithmetic: 1.78 us -> 4.62 us  [whole(): return grad.reshape(3, 3, CH, CH).astype(F32)]
where the time goes in v2:
time: 91.1 us; the launch traced here: 90.9 us
  Pallas kernels  83.5 us (92%)
  other arithmetic  4.62 us (5%)
  local copies, waits for them, and re-layouts  2.14 us (2%)
    pallas_call x1, Pallas kernels, per_device(): pl.pallas_call(functools.partial(kernel, grad_scale), out_shape=(jax.Shap...  83.5 us
    convert_element_type x2, other arithmetic, whole(): return grad.reshape(3, 3, CH, CH).astype(F32)  4.62 us
    unnamed x5, local copies, waits for them, and re-layouts  2.14 us

profile of v2, /device:TPU:1, one launch (start us, length us, event | category | flops | bytes accessed | tf_op | source)
XLA Modules:
  0.0 90.9 jit_solution(8202851216470915591)
XLA Ops:
  0.6 83.5 %shard_map.85 = (bf16[64,4,16,256]{3,2,1,0:T(8,128)(2,1)}, bf16[9,2,128,256]{3,2,1,0:T(8,128)(2,1)}, bf16[9,2,128,256]{3,2,1,0:T(8,128)(2,1)}) custom-call(bf16[64,4,16,256]{3,2,1,0:T(8,128)(2,1)} %bitcast.9, f32[64,256]{1,0:T(8,128)} %dec.1, bf16[2304,256]{1,0:T(8,128)(2,1)} %bitcast.14, bf16[3,3,256,256]{3,2,1,0:T(8,128)(2,1)} %kout_hbm.1, ...), custom_call_target="tpu_custom_call" | custom-call | tf_op jit(solution)/shard_map/pallas_call | solution.py:522
  84.1 0.0 copy-start.1
  84.1 3.0 %convert.2 = f32[3,3,256,256]{3,2,1,0:T(8,128)} convert(bf16[3,3,256,256]{3,2,1,0:T(8,128)(2,1)} %bitcast.13) | non-fusion elementwise | flops 589824 | bytes 3538944 | tf_op jit(solution)/shard_map/convert_element_type | solution.py:574
  87.1 0.0 copy-done.1
  87.1 0.0 copy-start
  87.1 1.6 %convert.3 = f32[3,3,256,256]{3,2,1,0:T(8,128)} convert(bf16[3,3,256,256]{3,2,1,0:T(8,128)(2,1)S(1)} %bitcast.12) | non-fusion elementwise | flops 589824 | bytes 3538944 | tf_op jit(solution)/shard_map/convert_element_type | solution.py:574
  88.7 0.8 copy-done
  89.6 1.3 %copy.10 = bf16[1,64,4,16,256]{4,3,2,1,0:T(8,128)(2,1)} copy(bf16[1,64,4,16,256]{4,3,2,1,0:T(8,128)(2,1)S(1)} %bitcast.11) | data formatting | bytes 4194304
Async XLA Ops:
  84.1 3.0 %copy-start.1 = (bf16[9,2,128,256]{3,2,1,0:T(8,128)(2,1)S(1)}, bf16[9,2,128,256]{3,2,1,0:T(8,128)(2,1)}, u32[]{:S(2)}) copy-start(bf16[9,2,128,256]{3,2,1,0:T(8,128)(2,1)} %get-tuple-element.8) | copy-start | bytes 3538948
  87.1 2.4 %copy-start = (bf16[64,4,16,256]{3,2,1,0:T(8,128)(2,1)S(1)}, bf16[64,4,16,256]{3,2,1,0:T(8,128)(2,1)}, u32[]{:S(2)}) copy-start(bf16[64,4,16,256]{3,2,1,0:T(8,128)(2,1)} %get-tuple-element.6) | copy-start | bytes 6291460

commit v3 on v2

--- a/solution.py
+++ b/solution.py
@@ -42,9 +42,9 @@
     grad_scale,
     x_hbm, dec, kin_hbm, kout_hbm, skip, cot_hbm,
     out_hbm, gin_hbm, gout_hbm,
-    xi, ci, kin, kout, ft, drv, adj, sb, dcb, ob, sc,
+    xi, ci, kin, kout, ft, drv, adj, sb, ob, sc,
     rx, rz, ry, incoming,
-    turned, acc, psend, precv, h1, h2, own, s1, r1, c1, r2, c2, r3, agb, pgb, fb,
+    turned, acc, psend, precv, h1, h2, own, r15, s1, r1, c1, r2, c2, r3, agb, pgb, fb,
     lsem, wsem, osem, gsem,
     hsend, hrecv, xsend, xrecv, zsend, zrecv, ysend, yrecv,
     psem, prem, s1s, s1r, s2s, s2r, s3s, s3r, a2s, a2r, a1s, a1r, pgs, pgr,
@@ -61,6 +61,11 @@
         if axis == "z":
             return (y_lo * 16 + k * 4 + lax.rem(tm, 4), row)
         return (lax.rem(k, 2) * 16 + lax.rem(tm, 16), (k // 2) * 2 + core)
+
+    def mate_2(axis_1, k_1, axis_2, k_2):
+        at = dict(pos)
+        at[axis_1], at[axis_2] = k_1, k_2
+        return (lax.rem(at["y"], 2) * 16 + at["z"] * 4 + at["x"], (at["y"] // 2) * 2 + core)
 
     def mates(axis):
         return [mate(axis, lax.rem(pos[axis] + d, LINE)) for d in (1, 2, 3)]
@@ -300,6 +305,11 @@
     widen_own(xi)
     load_kin.wait()
     conv(xi, kin, drv, 1, 1, 2)
+    load_kout.wait()
+    turn_kernel()
+    for load in loads[1]:
+        load.wait()
+    widen_own(ci)
     halo_arrived(0)
     widen(xi, 0)
     widen(xi, R + 1)
@@ -307,17 +317,11 @@
     end, decay = lax.fori_loop(0, T // UN, ends_forward, (zero_state, jnp.ones((1, CH), F32)))
     x_start(0, end.reshape(CELLS, CH), decay)
 
-    load_kout.wait()
-    turn_kernel()
-    for load in loads[1]:
-        load.wait()
-    widen_own(ci)
-    conv(ci, ft, adj, 1, 1, 1)
-    fx = x_to_z(0)
-    conv(ci, ft, adj, 2, 1, 1)
+    conv(ci, ft, adj, 1, 1, 2)
     halo_arrived(1)
     widen(ci, 0)
     widen(ci, R + 1)
+    fx = x_to_z(0)
     conv(ci, ft, adj, 0, 1, 1)
     fz = z_to_y(0)
     conv(ci, ft, adj, 3, 1, 1)
@@ -328,26 +332,19 @@
     halo_start(2)
 
     def turn(field, at):
-        def body(h, _):
-            turned[h] = field[h + at].reshape(T * W, CH).T
-            return 0
-
-        lax.fori_loop(0, R, body, 0)
+        for h in range(R):
+            turned[:, h * T * W:(h + 1) * T * W] = field[h + at].astype(BF16).reshape(T * W, CH).T
 
     def row_tap(g, other, i):
-        acc[g, i] = jnp.dot(turned[0], other[i].reshape(T * W, 3 * CH), preferred_element_type=F32)
-
-        def body(h, _):
-            acc[g, i] += jnp.dot(turned[h], other[h + i].reshape(T * W, 3 * CH), preferred_element_type=F32)
-            return 0
-
-        lax.fori_loop(1, R, body, 0)
+        acc[g, i] = jnp.dot(
+            turned[...], other[i:i + R].reshape(R * T * W, 3 * CH), preferred_element_type=F32
+        )
 
     def adjoints(n, v):
         for u in range(UN):
             t = T - 1 - (n * UN + u)
             a = adj[:, t] + v
-            dcb[:, t] = (sc[pl.ds(t, 1), :] * a).astype(BF16)
+            drv[:, t] = sc[pl.ds(t, 1), :] * a
             v = decay_at(t) * a
         return v
 
@@ -403,8 +400,19 @@
             total = (c2[g, q] + r3[g, q, 1]) + (r3[g, q, 0] + r3[g, q, 2])
             mine = agb.at[g, q, me_1, me_2]
             mine[...] = (total * grad_scale).astype(BF16)
-            for device in mates(axis_2):
+            for device in plane if wide else mates(axis_2):
                 remote(mine, mine, a2s.at[g, q], a2r.at[g, q], device).start()
+
+        wide = g == 1
+        plane = [
+            mate_2(axis_1, lax.rem(me_1 + d, LINE), axis_2, lax.rem(me_2 + e, LINE))
+            for d in range(LINE) for e in range(LINE) if d + e > 0
+        ]
+
+        def share_wide():
+            many = r15.at[...]
+            remote(many, many, a2s.at[g, q], a2r.at[g, q], pair).wait()
+            hand_over.start()
 
         def widen_out():
             three = agb.at[g, q, 0, pl.ds(0, 3)]
@@ -435,6 +443,8 @@
             unpack(pgb, 1 - core)
             out(g, q).start()
 
+        if wide:
+            return [begin, scatter, second, cross, gather, share_wide, lambda: None, last]
         return [begin, scatter, second, cross, gather, widen_out, share, last]
 
     def out(g, q):
@@ -480,7 +490,7 @@
     run((ro[2], 1), (ro[0], 2))
     from_y(1, bz, bx)
     lax.fori_loop(0, T // UN, adjoints, incoming[1].reshape(R, W, CH))
-    turn(dcb, 0)
+    turn(drv, 0)
     row_tap(1, xi, 0)
     run((ri[0], 0), (ro[1], 2), (ro[2], 2), (ro[0], 3))
     row_tap(1, xi, 1)
@@ -509,6 +519,29 @@
     for g in range(2):
         for q in range(3):
             out(g, q).wait()
+
+
+def finish(y_in, gin_in, gout_in, y_out, gin_out, gout_out, yb, gb, gf, ysem, gsem, ydone, gdone):
+    grads = ((gout_in, gout_out), (gin_in, gin_out))
+    y_loads = [pltpu.make_async_copy(y_in.at[n * FB:(n + 1) * FB], yb.at[n], ysem.at[n]) for n in range(NB)]
+    y_stores = [pltpu.make_async_copy(yb.at[n], y_out.at[n * FB:(n + 1) * FB], ydone.at[n]) for n in range(NB)]
+    g_loads = [[pltpu.make_async_copy(grads[g][0].at[3 * q:3 * q + 3], gb.at[g, q], gsem.at[g, q]) for q in range(3)] for g in range(2)]
+    g_stores = [[pltpu.make_async_copy(gf.at[g, q], grads[g][1].at[3 * q:3 * q + 3], gdone.at[g, q]) for q in range(3)] for g in range(2)]
+    for g in range(2):
+        for q in range(3):
+            g_loads[g][q].start()
+    for load in y_loads:
+        load.start()
+    for g in range(2):
+        for q in range(3):
+            g_loads[g][q].wait()
+            gf[g, q] = gb[g, q].astype(F32)
+            g_stores[g][q].start()
+    for load, store in zip(y_loads, y_stores):
+        load.wait()
+        store.start()
+    for store in y_stores + g_stores[0] + g_stores[1]:
+        store.wait()
 
 
 def per_device(inputs, decays, in_kernel, out_kernel, skip, cotangent):
@@ -534,19 +567,19 @@
             V((R, T, W, CH), F32),
             V((R + 2, T, W, CH), BF16),
             V((R, T, W, CH), BF16),
-            V((R, T, W, CH), BF16),
             V((T, CH), F32),
             V((2, 4, MSG, CH), F32),
             V((2, 4, MSG, CH), F32),
             V((2, 2, CELLS, CH), F32),
             V((2, CELLS, CH), F32),
-            V((R, CH, T * W), BF16),
+            V((CH, R * T * W), BF16),
             V((2, 3, CH, 3 * CH), F32),
             V((2, 3, 384, CH), BF16),
             V((2, 3, 384, CH), BF16),
             V((384, CH), F32),
             V((LINE, 96, CH), F32),
             V((2, 3, 96, CH), F32),
+            V((15,) + CHUNK, BF16),
             V((2, 3, LINE, 96, CH), BF16),
             V((2, 3, 3, 96, CH), BF16),
             V((2, 3, LINE) + CHUNK, F32),
@@ -570,10 +603,21 @@
         skip.reshape(1, CH), cotangent.reshape(T, R, W, CH),
     )
 
-    def whole(grad):
-        return grad.reshape(3, 3, CH, CH).astype(F32)
-
-    return outputs.reshape(inputs.shape), whole(in_grad), whole(out_grad)
+    grad = jax.ShapeDtypeStruct((9, 2, 128, CH), F32)
+    outputs, in_grad, out_grad = pl.pallas_call(
+        finish,
+        out_shape=(jax.ShapeDtypeStruct((T, R, W, CH), BF16), grad, grad),
+        in_specs=[pl.BlockSpec(memory_space=pltpu.HBM)] * 3,
+        out_specs=(anywhere,) * 3,
+        scratch_shapes=[
+            V((NB, FB, R, W, CH), BF16),
+            V((2, 3, 3, 2, 128, CH), BF16),
+            V((2, 3, 3, 2, 128, CH), F32),
+            dma((NB,)), dma((2, 3)), dma((NB,)), dma((2, 3)),
+        ],
+        compiler_params=pltpu.CompilerParams(vmem_limit_bytes=62 * 1024 * 1024),
+    )(outputs, in_grad, out_grad)
+    return outputs.reshape(inputs.shape), in_grad.reshape(3, 3, CH, CH), out_grad.reshape(3, 3, CH, CH)
 
 
 def solution(mesh):

time: 91.1 us -> 84.9 us (0.932)
  other arithmetic: 4.62 us -> 0 us
  local copies, waits for them, and re-layouts: 2.14 us -> 0 us
    convert_element_type x2 -> x0, other arithmetic: 4.62 us -> none  [whole(): return grad.reshape(3, 3, CH, CH).astype(F32)]
    pallas_call x0 -> x1, Pallas kernels: none -> 4.07 us  [per_device(): pl.pallas_call(finish, out_shape=(jax.ShapeDtypeStruct((T, R, W, CH), BF1...]
    pallas_call x1, Pallas kernels: 83.5 us -> 79.9 us  [per_device(): pl.pallas_call(functools.partial(kernel, grad_scale), out_shape=(jax.Shap...]
    unnamed x5 -> x0, local copies, waits for them, and re-layouts: 2.14 us -> none
where the time goes in v3:
time: 84.9 us; the launch traced here: 84.8 us
  Pallas kernels  84 us (99%)
    pallas_call x1, Pallas kernels, per_device(): pl.pallas_call(functools.partial(kernel, grad_scale), out_shape=(jax.Shap...  79.9 us
    pallas_call x1, Pallas kernels, per_device(): pl.pallas_call(finish, out_shape=(jax.ShapeDtypeStruct((T, R, W, CH), BF1...  4.07 us

profile of v3, /device:TPU:1, one launch (start us, length us, event | category | flops | bytes accessed | tf_op | source)
XLA Modules:
  0.0 84.8 jit_solution(6645746555205088887)
XLA Ops:
  0.6 79.9 %shard_map.85 = (bf16[64,4,16,256]{3,2,1,0:T(8,128)(2,1)}, bf16[9,2,128,256]{3,2,1,0:T(8,128)(2,1)}, bf16[9,2,128,256]{3,2,1,0:T(8,128)(2,1)}) custom-call(bf16[64,4,16,256]{3,2,1,0:T(8,128)(2,1)} %bitcast.7, f32[64,256]{1,0:T(8,128)} %dec.1, bf16[2304,256]{1,0:T(8,128)(2,1)} %bitcast.9, bf16[3,3,256,256]{3,2,1,0:T(8,128)(2,1)} %kout_hbm.1, ...), custom_call_target="tpu_custom_call" | custom-call | tf_op jit(solution)/shard_map/pallas_call | solution.py:555
  80.6 4.1 %shard_map.86 = (bf16[64,4,16,256]{3,2,1,0:T(8,128)(2,1)}, f32[9,2,128,256]{3,2,1,0:T(8,128)}, f32[9,2,128,256]{3,2,1,0:T(8,128)}) custom-call(bf16[64,4,16,256]{3,2,1,0:T(8,128)(2,1)} %get-tuple-element.9.y_in, bf16[9,2,128,256]{3,2,1,0:T(8,128)(2,1)} %get-tuple-element.10.gin_in, bf16[9,2,128,256]{3,2,1,0:T(8,128)(2,1)} %get-tuple-element.11.gout_in), custom_call_target="tpu_custom_call" | custom-call | tf_op jit(solution)/shard_map/pallas_call | solution.py:607

commit v4 on v3

--- a/solution.py
+++ b/solution.py
@@ -208,7 +208,7 @@
 
         lax.fori_loop(1, R + 1, body, 0)
 
-    UN = 4
+    UN = 8
 
     def decay_at(t):
         return dec[pl.ds(t, 1), :]
@@ -323,10 +323,10 @@
     widen(ci, R + 1)
     fx = x_to_z(0)
     conv(ci, ft, adj, 0, 1, 1)
-    fz = z_to_y(0)
     conv(ci, ft, adj, 3, 1, 1)
     lead = lax.fori_loop(0, T // UN, ends_backward, zero_state)
     x_start(1, lead.reshape(CELLS, CH), decay)
+    fz = z_to_y(0)
     from_y(0, fz, fx)
     lax.fori_loop(0, T // UN, states, incoming[0].reshape(R, W, CH))
     halo_start(2)
@@ -477,15 +477,15 @@
         store.start()
         return store
 
+    bx = x_to_z(1)
     turn(sb, 1)
     row_tap(0, ci, 2)
     run((ro[0], 0))
-    bx = x_to_z(1)
     row_tap(0, ci, 1)
     run((ro[1], 0), (ro[0], 1))
     row_tap(0, ci, 0)
+    bz = z_to_y(1)
     run((ro[2], 0), (ro[1], 1))
-    bz = z_to_y(1)
     stores = [mix(1)]
     run((ro[2], 1), (ro[0], 2))
     from_y(1, bz, bx)

time: 84.9 us -> 83.9 us (0.988)
  Pallas kernels: 84 us -> 82.9 us
    pallas_call x1, Pallas kernels: 79.9 us -> 78.8 us  [per_device(): pl.pallas_call(functools.partial(kernel, grad_scale), out_shape=(jax.Shap...]
where the time goes in v4:
time: 83.9 us; the launch traced here: 83.7 us
  Pallas kernels  82.9 us (99%)
    pallas_call x1, Pallas kernels, per_device(): pl.pallas_call(functools.partial(kernel, grad_scale), out_shape=(jax.Shap...  78.8 us
    pallas_call x1, Pallas kernels, per_device(): pl.pallas_call(finish, out_shape=(jax.ShapeDtypeStruct((T, R, W, CH), BF1...  4.07 us

profile of v4, /device:TPU:1, one launch (start us, length us, event | category | flops | bytes accessed | tf_op | source)
XLA Modules:
  0.0 83.7 jit_solution(6191510381933943975)
XLA Ops:
  0.6 78.8 %shard_map.85 = (bf16[64,4,16,256]{3,2,1,0:T(8,128)(2,1)}, bf16[9,2,128,256]{3,2,1,0:T(8,128)(2,1)}, bf16[9,2,128,256]{3,2,1,0:T(8,128)(2,1)}) custom-call(bf16[64,4,16,256]{3,2,1,0:T(8,128)(2,1)} %bitcast.7, f32[64,256]{1,0:T(8,128)} %dec.1, bf16[2304,256]{1,0:T(8,128)(2,1)} %bitcast.9, bf16[3,3,256,256]{3,2,1,0:T(8,128)(2,1)} %kout_hbm.1, ...), custom_call_target="tpu_custom_call" | custom-call | tf_op jit(solution)/shard_map/pallas_call | solution.py:555
  79.5 4.1 %shard_map.86 = (bf16[64,4,16,256]{3,2,1,0:T(8,128)(2,1)}, f32[9,2,128,256]{3,2,1,0:T(8,128)}, f32[9,2,128,256]{3,2,1,0:T(8,128)}) custom-call(bf16[64,4,16,256]{3,2,1,0:T(8,128)(2,1)} %get-tuple-element.9.y_in, bf16[9,2,128,256]{3,2,1,0:T(8,128)(2,1)} %get-tuple-element.10.gin_in, bf16[9,2,128,256]{3,2,1,0:T(8,128)(2,1)} %get-tuple-element.11.gout_in), custom_call_target="tpu_custom_call" | custom-call | tf_op jit(solution)/shard_map/pallas_call | solution.py:607
